TPU v7x, 256 devices: a whole 4x4x8 slice. The times are simulated.
256 devices in a mesh: seq: 16 (over y_lo, z), dp: 16 (over x, y_hi, core).
Axes of the slice: x: 4, y: 4 (y_hi: 2, y_lo: 2; y = y_hi * 2 + y_lo), z: 8, core: 2. Of those that a mesh axis runs over, the one named last changes fastest.
Arguments:
- layer_rows: bfloat16 [16, 2048, 1024], P('dp', 'seq'), may hold values from -6 to 6
- doc_ids: int32 [16, 2048], P('dp', 'seq'), may hold values from 0 to 5, never falling along the last dimension, each value on 1 to 1024 neighbouring positions
- packing: int32 [16, 16], P('dp'), may hold values from 0 to 15, each once within a row
- norm_gain: float32 [1024], replicated, may hold values from 0.1 to 1.9
- w_qkv: bfloat16 [1024, 3072], replicated, may hold values from -0.1875 to 0.1875
- d_attn: bfloat16 [16, 2048, 1024], P('dp', 'seq'), may hold values from -6 to 6
Outputs:
- d_input: bfloat16 [16, 2048, 1024], P('dp', 'seq')
- w_grad: float32 [1024, 3072], P('seq')
Inputs may be any that keep to these rules, and one draw needn't show every extreme that they name: `doc_ids`: in each group the song numbers never fall along the initial order; every number occurs, and one song spans exactly 1024 frames. `packing`: each group's row names every block number once.
All inputs are finite; a program needn't handle non-finite values.
Results may differ from a plain program's by a relative error of at most 0.024.
Values may be sent and summed in bfloat16 or wider, within the bound.
No kernel may reach another device: no remote copies, remote signals or barrier semaphores. Data moves between devices by JAX's collectives and lax.ppermute only.
A program may use at most 128 MiB of HBM per device.

v0:
```python
import math
import jax
import jax.numpy as jnp
from jax import lax
from jax.sharding import PartitionSpec as P

HEADS = 8
HEAD = 128
BLOCK = 128


def rounded(value):
    return lax.optimization_barrier(value.astype(jnp.bfloat16)).astype(jnp.float32)


def normalize(frames, norm_gain):
    values = frames.astype(jnp.float32)
    inverse = lax.rsqrt(jnp.mean(values * values, axis=-1, keepdims=True) + 1e-05)
    unit_rows = values * inverse
    return (inverse, unit_rows, (unit_rows * norm_gain).astype(jnp.bfloat16))


def body(layer_rows, doc_ids, packing, norm_gain, w_qkv, d_attn):
    shards = lax.axis_size("seq")
    my_index = lax.axis_index("seq")
    frames = layer_rows[0]
    tok_rows = frames.shape[0]
    head_cols = HEADS * HEAD
    total_keys = tok_rows * shards
    block_order = packing[0]
    key_pos = (block_order[:, None] * BLOCK + jnp.arange(BLOCK, dtype=jnp.int32)[None, :]).reshape(
        total_keys
    )
    first_own = my_index * tok_rows
    my_pos = lax.dynamic_slice_in_dim(key_pos, first_own, tok_rows, 0)
    doc_low = doc_ids[0].astype(jnp.bfloat16)
    pieces = (
        lax.all_gather(frames, "seq", axis=0, tiled=True),
        lax.all_gather(doc_low, "seq", axis=0, tiled=True),
    )
    length = pieces[0].shape[0]
    inside = (my_pos >= 0) & (my_pos < length)
    clipped = jnp.clip(my_pos, 0, length - 1)
    new_rows = jnp.where(
        inside[:, None], jnp.take(pieces[0], clipped, axis=0), jnp.zeros_like(frames)
    )
    new_docs = jnp.where(inside, jnp.take(pieces[1], clipped, axis=0), jnp.zeros_like(doc_low))
    inverse, unit_rows, normed = normalize(new_rows, norm_gain)
    projected = jnp.dot(normed, w_qkv, preferred_element_type=jnp.float32).astype(jnp.bfloat16)
    queries = projected[:, :head_cols]
    all_keys, all_values, key_docs_low = (
        lax.all_gather(projected[:, head_cols : 2 * head_cols], "seq", axis=0, tiled=True),
        lax.all_gather(projected[:, 2 * head_cols :], "seq", axis=0, tiled=True),
        lax.all_gather(new_docs, "seq", axis=0, tiled=True),
    )
    key_docs = key_docs_low.astype(jnp.int32)
    my_docs = lax.dynamic_slice_in_dim(key_docs, first_own, tok_rows, 0)
    factor = 1.0 / math.sqrt(HEAD)
    q_heads = queries.reshape(tok_rows, HEADS, HEAD)
    grad_heads = d_attn[0].reshape(tok_rows, HEADS, HEAD)
    group_count = total_keys // total_keys

    def key_slab(group_idx):
        first_key = group_idx * total_keys
        slab_keys = all_keys.reshape(total_keys, HEADS, HEAD)
        slab_values = all_values.reshape(total_keys, HEADS, HEAD)
        allowed = (my_docs[:, None] == key_docs[None, :]) & (key_pos[None, :] <= my_pos[:, None])
        return (first_key, slab_keys, slab_values, allowed)

    def exp_scores(query_part, slab_keys, allowed):
        scores = (
            jnp.einsum("qhd,khd->hqk", query_part, slab_keys, preferred_element_type=jnp.float32)
            * factor
        )
        return jnp.where(allowed[None], jnp.exp(scores), jnp.float32(0.0))

    def add_denominator(group_idx, running):
        first_key, slab_keys, slab_values, allowed = key_slab(group_idx)
        return running + jnp.sum(exp_scores(q_heads, slab_keys, allowed), axis=-1)

    denominator = lax.fori_loop(
        0, group_count, add_denominator, jnp.zeros((HEADS, tok_rows), jnp.float32)
    )

    def probabilities(slab_keys, allowed):
        attn_prob = exp_scores(q_heads, slab_keys, allowed) / denominator[:, :, None]
        return (attn_prob, attn_prob.astype(jnp.bfloat16))

    def add_output(group_idx, running):
        first_key, slab_keys, slab_values, allowed = key_slab(group_idx)

        def compute():
            attn_prob, prob_low = probabilities(slab_keys, allowed)
            return jnp.einsum(
                "hqk,khd->qhd", prob_low, slab_values, preferred_element_type=jnp.float32
            )

        return running + compute()

    outputs = lax.fori_loop(
        0, group_count, add_output, jnp.zeros((tok_rows, HEADS, HEAD), jnp.float32)
    )
    row_delta = jnp.sum(grad_heads.astype(jnp.float32) * outputs, axis=-1).T

    def slab_backward(slab_keys, slab_values, allowed):
        attn_prob, prob_low = probabilities(slab_keys, allowed)
        grad_prob = jnp.einsum(
            "qhd,khd->hqk", grad_heads, slab_values, preferred_element_type=jnp.float32
        )
        dscore = (attn_prob * (grad_prob - row_delta[:, :, None])).astype(jnp.bfloat16)
        dq_part = (
            jnp.einsum("hqk,khd->qhd", dscore, slab_keys, preferred_element_type=jnp.float32)
            * factor
        )
        return (dq_part, dscore, prob_low)

    def add_grads(group_idx, running):
        dq_sum, kv_grads = running
        first_key, slab_keys, slab_values, allowed = key_slab(group_idx)

        def compute():
            dq_part, dscore, prob_low = slab_backward(slab_keys, slab_values, allowed)
            dk_part = (
                jnp.einsum("hqk,qhd->khd", dscore, q_heads, preferred_element_type=jnp.float32)
                * factor
            )
            dv_part = jnp.einsum(
                "hqk,qhd->khd", prob_low, grad_heads, preferred_element_type=jnp.float32
            )
            return (
                dq_part,
                jnp.concatenate(
                    [
                        dk_part.reshape(total_keys, head_cols),
                        dv_part.reshape(total_keys, head_cols),
                    ],
                    axis=1,
                ),
            )

        dq_part, kv_part = compute()
        return (dq_sum + dq_part, kv_part)

    dq_sum, kv_grads = lax.fori_loop(
        0,
        group_count,
        add_grads,
        (
            jnp.zeros((tok_rows, HEADS, HEAD), jnp.float32),
            jnp.zeros((total_keys, 2 * head_cols), jnp.float32),
        ),
    )
    summed = lax.psum_scatter(
        rounded(kv_grads).astype(jnp.bfloat16), "seq", scatter_dimension=0, tiled=True
    ).astype(jnp.float32)
    grad_qkv = jnp.concatenate([dq_sum.reshape(tok_rows, head_cols), summed], axis=1).astype(
        jnp.bfloat16
    )
    d_normed = lax.dot_general(
        grad_qkv, w_qkv, (((1,), (1,)), ((), ())), preferred_element_type=jnp.float32
    )
    gained = d_normed * norm_gain
    d_frames = (
        inverse * (gained - unit_rows * jnp.mean(gained * unit_rows, axis=-1, keepdims=True))
    ).astype(jnp.bfloat16)
    w_part = lax.psum_scatter(
        rounded(
            lax.dot_general(
                normed, grad_qkv, (((0,), (0,)), ((), ())), preferred_element_type=jnp.float32
            )
        ).astype(jnp.bfloat16),
        "seq",
        scatter_dimension=0,
        tiled=True,
    )
    w_total = lax.psum(w_part, "dp").astype(jnp.float32)
    w_grad = w_total * (1.0 / math.sqrt(total_keys * lax.axis_size("dp")))
    return (d_frames[None], w_grad)


def solution(mesh):
    return jax.shard_map(
        body,
        mesh=mesh,
        in_specs=(
            P("dp", "seq", None),
            P("dp", "seq"),
            P("dp", None),
            P(),
            P(),
            P("dp", "seq", None),
        ),
        out_specs=(P("dp", "seq", None), P("seq", None)),
        check_vma=False,
    )
```

profile of v0, /device:TPU:1, one launch (start us, length us, event | category | flops | bytes accessed | tf_op | source)
XLA Modules:
  0.0 635.3 jit_solution(11670641613337491043)
XLA Ops:
  7.2 0.0 all-gather.11.cloned.1.call-start
  7.2 0.7 all-gather.11.cloned.1.call-update
  7.9 0.0 all-gather.7.cloned.1.call-start
  7.9 0.7 multiply_bitcast_fusion
  8.6 0.1 add_bitcast_fusion
  8.7 0.1 compare_and_fusion.2
  8.8 71.3 %all-gather.11.cloned.1.call-done = bf16[1,2048,1024]{2,1,0:T(8,128)(2,1)} async-done(((bf16[1,128,1024]{2,1,0:T(8,128)(2,1)}), bf16[1,2048,1024]{2,1,0:T(8,128)(2,1)}) %all-gather.11.cloned.1.call-update) | async-done | bytes 4194320 | tf_op jit(solution)/shard_map/all_gather | solution.py:38
  80.1 3.8 gather_fusion
  83.8 0.2 fusion.24
  84.1 3.9 convolution_convert_fusion.2
  88.1 0.8 fusion.32
  88.9 0.0 all-gather.7.cloned.1.call-update
  88.9 0.0 all-gather.9.cloned.1.call-start
  89.0 0.7 all-gather.9.cloned.1.call-update
  89.7 0.0 reduce-scatter.7.cloned.1.call-start
  89.7 25.4 %all-gather.1 = bf16[1,2048]{1,0:T(2,128)(2,1)S(1)} all-gather(bf16[1,128]{1,0:T(2,128)(2,1)S(1)} %convert_element_type.50), channel_id=3, replica_groups=mesh['seq'=16,'dp'=16] {'seq'}, dimensions={1}, use_global_device_ids=true | all-gather | bytes 4352 | tf_op jit(solution)/shard_map/all_gather | solution.py:39
  115.2 1.3 gather_fusion.1
  116.5 24.9 %all-gather.2 = bf16[16,1,128]{2,1,0:T(2,128)(2,1)S(1)} all-gather(bf16[1,1,128]{2,1,0:T(2,128)(2,1)S(1)} %select_bitcast_fusion), channel_id=1, replica_groups=mesh['seq'=16,'dp'=16] {'seq'}, dimensions={0}, use_global_device_ids=true | all-gather | bytes 4352 | tf_op jit(solution)/shard_map/all_gather | solution.py:54
  141.5 0.1 dynamic_slice.7
  141.5 0.2 copy.28
  141.7 0.3 compare_and_fusion
  142.0 0.2 copy.40
  142.2 21.2 %all-gather.7.cloned.1.call-done = bf16[2048,1024]{1,0:T(8,128)(2,1)} async-done(((bf16[128,1024]{1,0:T(8,128)(2,1)}), bf16[2048,1024]{1,0:T(8,128)(2,1)}) %all-gather.7.cloned.1.call-update) | async-done | bytes 4194320 | tf_op jit(solution)/shard_map/all_gather | solution.py:52
  163.4 6.5 %copy.39 = bf16[2048,1024]{0,1:T(8,128)(2,1)} copy(bf16[2048,1024]{1,0:T(8,128)(2,1)} %all-gather.7.cloned.1.call-done) | data formatting | bytes 8388608 | tf_op jit(solution)/shard_map/while/body/eval_jaxpr/reshape | solution.py:65
  169.9 5.1 fusion.2
  175.0 3.2 copy-done
  178.2 4.5 convolution_convert_fusion.1
  182.8 55.8 %all-gather.9.cloned.1.call-done = bf16[2048,1024]{1,0:T(8,128)(2,1)} async-done(((bf16[128,1024]{1,0:T(8,128)(2,1)}), bf16[2048,1024]{1,0:T(8,128)(2,1)}) %all-gather.9.cloned.1.call-update) | async-done | bytes 4194320 | tf_op jit(solution)/shard_map/all_gather | solution.py:53
  238.5 6.5 %copy.41 = bf16[2048,1024]{0,1:T(8,128)(2,1)} copy(bf16[2048,1024]{1,0:T(8,128)(2,1)} %all-gather.9.cloned.1.call-done) | data formatting | bytes 8388608 | tf_op jit(solution)/shard_map/while/body/eval_jaxpr/reshape | solution.py:66
  245.0 7.3 %fusion.13 = f32[128,8]{0,1:T(8,128)S(1)} fusion(bf16[2048,8,128]{0,2,1:T(8,128)(2,1)} %bitcast.50, bf16[128,8,128]{0,2,1:T(8,128)(2,1)S(1)} %bitcast.59, f32[8,128,2048]{2,1,0:T(8,128)} %copy-done, f32[8,128]{1,0:T(8,128)S(1)} %get-tuple-element.73, pred[128,2048]{1,0:T(8,128)(4,1)S(1)} %compare_and_fusion), kind=kOutput, calls=%fused_computation.20 | convolution fusion | flops 545651712 | bytes 13115392 | tf_op jit(solution)/shard_map/while/body/eval_jaxpr/hqk,khd->qhd/dot_general | solution.py:94
  252.3 5.2 fusion
  257.6 2.0 copy-done.2
  259.5 3.2 multiply_convert_fusion
  262.7 8.3 %pad_maximum_fusion = bf16[2048,2048]{0,1:T(8,128)(2,1)} fusion(bf16[2048,1024]{0,1:T(8,128)(2,1)} %bitcast.52, bf16[2048,1024]{0,1:T(8,128)(2,1)} %bitcast.49), kind=kLoop, calls=%fused_computation.2 | loop fusion | flops 16777216 | bytes 16777216 | tf_op jit(solution)/shard_map/while/body/eval_jaxpr/concatenate | solution.py:132
  271.1 12.2 %copy.37 = bf16[2048,2048]{1,0:T(8,128)(2,1)} copy(bf16[2048,2048]{0,1:T(8,128)(2,1)} %pad_maximum_fusion) | data formatting | bytes 16777216
  283.3 0.0 reduce-scatter.7.cloned.1.call-update
  283.3 0.3 reduce-scatter.5.cloned.1.call-start
  283.6 4.7 fusion.12
  288.3 103.2 %reduce-scatter.7.cloned.1.call-done = bf16[128,2048]{1,0:T(8,128)(2,1)} async-done(((bf16[2048,2048]{1,0:T(8,128)(2,1)}), bf16[128,2048]{1,0:T(8,128)(2,1)}) %reduce-scatter.7.cloned.1.call-update) | async-done | bytes 524304
  391.6 1.3 copy.38
  392.9 4.6 convolution_convert_fusion
  397.5 0.0 reduce-scatter.5.cloned.1.call-update
  397.6 0.0 all-reduce.2.cloned.1.call-start
  397.6 5.1 fusion.20
  402.7 71.0 %reduce-scatter.5.cloned.1.call-done = bf16[64,3072]{1,0:T(8,128)(2,1)} async-done(((bf16[1024,3072]{1,0:T(8,128)(2,1)}), bf16[64,3072]{1,0:T(8,128)(2,1)}) %reduce-scatter.5.cloned.1.call-update) | async-done | bytes 393232 | tf_op jit(solution)/shard_map/reduce_scatter | solution.py:166
  473.8 0.9 fusion.25
  474.7 151.8 %all-reduce.2.cloned.1.call-done = bf16[64,3072]{1,0:T(8,128)(2,1)} async-done(((bf16[64,3072]{1,0:T(8,128)(2,1)}), bf16[64,3072]{1,0:T(8,128)(2,1)}) %all-reduce.2.cloned.1.call-update) | async-done | bytes 393232 | tf_op jit(solution)/shard_map/psum | solution.py:176
  626.5 1.9 convert_multiply_fusion
  (20 shorter events, 0.1 us)
Async XLA Ops:
  7.2 72.9 %all-gather.11.cloned.1.call-start = ((), (), s32[]{:S(2)}) async-start(), calls=%async_computation.6 | async-start | bytes 4456448 | tf_op jit(solution)/shard_map/all_gather | solution.py:38
  7.9 155.5 %all-gather.7.cloned.1.call-start = ((), (), s32[]{:S(2)}) async-start(), calls=%async_computation.2 | async-start | bytes 4456448 | tf_op jit(solution)/shard_map/all_gather | solution.py:52
  84.1 5.6 copy-start.5
  84.1 57.4 %copy-start.3 = (bf16[1,128,1024]{2,1,0:T(8,128)(2,1)S(1)}, bf16[1,128,1024]{2,1,0:T(8,128)(2,1)}, u32[]{:S(2)}) copy-start(bf16[1,128,1024]{2,1,0:T(8,128)(2,1)} %param.11) | copy-start | bytes 786436
  88.9 149.6 %all-gather.9.cloned.1.call-start = ((), (), s32[]{:S(2)}) async-start(), calls=%async_computation.3 | async-start | bytes 4456448 | tf_op jit(solution)/shard_map/all_gather | solution.py:53
  89.7 301.9 %reduce-scatter.7.cloned.1.call-start = ((), (), s32[]{:S(2)}) async-start(), calls=%async_computation.7 | async-start | bytes 8912896
  175.0 3.2 copy-start
  245.0 7.3 %copy-start.1 = (f32[8,128,2048]{2,1,0:T(8,128)S(1)}, f32[8,128,2048]{2,1,0:T(8,128)}, u32[]{:S(2)}) copy-start(f32[8,128,2048]{2,1,0:T(8,128)} %copy-done) | copy-start | bytes 25165828
  257.6 2.0 copy-start.2
  283.3 109.6 %copy-start.4 = (f32[1024]{0:T(1024)S(1)}, f32[1024]{0:T(1024)}, u32[]{:S(2)}) copy-start(f32[1024]{0:T(1024)} %param.9) | copy-start | bytes 12292
  283.3 190.4 %reduce-scatter.5.cloned.1.call-start = ((), (), s32[]{:S(2)}) async-start(), calls=%async_computation.4 | async-start | bytes 6684672 | tf_op jit(solution)/shard_map/reduce_scatter | solution.py:166
  397.6 228.9 %all-reduce.2.cloned.1.call-start = ((), (), s32[]{:S(2)}) async-start(), calls=%async_computation.5 | async-start | bytes 786432 | tf_op jit(solution)/shard_map/psum | solution.py:176
Sparse Core Ops, SparseCore 0:
  9.8 70.2 all-gather.10
  89.0 74.2 all-gather.6
  165.7 72.7 all-gather.8
  283.5 108.0 reduce-scatter.6
  397.7 76.0 reduce-scatter.4
  476.2 150.2 all-reduce.1
where the time goes:
time: 636 us; the launch traced here: 635 us
  waiting for transfers between devices  476 us (75%)
  blocking collectives  50.4 us (8%)
  matrix products  43.7 us (7%)
  local copies, waits for them, and re-layouts  38.1 us (6%)
  between operations  14.3 us (2%)
  other arithmetic  12.6 us (2%)
    psum x1, waiting for transfers between devices, body(): w_total = lax.psum(w_part, 'dp').astype(jnp.float32)  152 us
    unnamed x7, waiting for transfers between devices  105 us
    all_gather x1, waiting for transfers between devices, body(): lax.all_gather(frames, 'seq', axis=0, tiled=True)  71.3 us
    reduce_scatter x1, waiting for transfers between devices, body(): lax.psum_scatter(rounded(lax.dot_general(normed, grad_qkv, (((0,), (0,)),...  71 us
    all_gather x1, waiting for transfers between devices, body(): lax.all_gather(projected[:, 2 * head_cols:], 'seq', axis=0, tiled=True)  55.8 us
    all_gather x1, blocking collectives, body(): lax.all_gather(doc_low, 'seq', axis=0, tiled=True)  25.4 us
    all_gather x1, blocking collectives, body(): lax.all_gather(new_docs, 'seq', axis=0, tiled=True)  24.9 us
    all_gather x1, waiting for transfers between devices, body(): lax.all_gather(projected[:, head_cols:2 * head_cols], 'seq', axis=0, tile...  21.2 us
  transfers between devices with their start and end apart: 6, of which 6 were waited for; matrix products, arithmetic and copies ran while one was open for 5% of the time, Pallas kernels for 0%

commit v1 on v0

--- a/solution.py
+++ b/solution.py
@@ -7,6 +7,11 @@
 HEADS = 8
 HEAD = 128
 BLOCK = 128
+
+
+def add_all(x, axis):
+    shards = lax.all_gather(x, axis)
+    return jnp.sum(shards, axis=0)
 
 
 def rounded(value):
@@ -173,7 +178,7 @@
         scatter_dimension=0,
         tiled=True,
     )
-    w_total = lax.psum(w_part, "dp").astype(jnp.float32)
+    w_total = add_all(w_part, "dp").astype(jnp.float32)
     w_grad = w_total * (1.0 / math.sqrt(total_keys * lax.axis_size("dp")))
     return (d_frames[None], w_grad)
 

time: 636 us -> 564 us (0.89)
  waiting for transfers between devices: 476 us -> 401 us
    psum x1 -> x0, waiting for transfers between devices: 152 us -> none  [body(): w_total = lax.psum(w_part, 'dp').astype(jnp.float32)]
    all_gather x0 -> x1, waiting for transfers between devices: none -> 71.8 us  [add_all(): shards = lax.all_gather(x, axis)]
where the time goes in v1:
time: 564 us; the launch traced here: 563 us
  waiting for transfers between devices  401 us (71%)
  blocking collectives  50.4 us (9%)
  matrix products  43.7 us (8%)
  local copies, waits for them, and re-layouts  38.1 us (7%)
  other arithmetic  15.6 us (3%)
  between operations  14.3 us (3%)
    unnamed x7, waiting for transfers between devices  105 us
    reduce_scatter x1, waiting for transfers between devices, body(): lax.psum_scatter(rounded(lax.dot_general(normed, grad_qkv, (((0,), (0,)),...  76.1 us
    all_gather x1, waiting for transfers between devices, add_all(): shards = lax.all_gather(x, axis)  71.8 us
    all_gather x1, waiting for transfers between devices, body(): lax.all_gather(frames, 'seq', axis=0, tiled=True)  71.3 us
    all_gather x1, waiting for transfers between devices, body(): lax.all_gather(projected[:, 2 * head_cols:], 'seq', axis=0, tiled=True)  55.8 us
    all_gather x1, blocking collectives, body(): lax.all_gather(doc_low, 'seq', axis=0, tiled=True)  25.4 us
    all_gather x1, blocking collectives, body(): lax.all_gather(new_docs, 'seq', axis=0, tiled=True)  24.9 us
    all_gather x1, waiting for transfers between devices, body(): lax.all_gather(projected[:, head_cols:2 * head_cols], 'seq', axis=0, tile...  21.2 us
  transfers between devices with their start and end apart: 6, of which 6 were waited for; matrix products, arithmetic and copies ran while one was open for 5% of the time, Pallas kernels for 0%

profile of v1, /device:TPU:1, one launch (start us, length us, event | category | flops | bytes accessed | tf_op | source)
XLA Modules:
  0.0 563.4 jit_solution(12293362231171546904)
XLA Ops:
  7.2 0.0 all-gather.13.cloned.1.call-start
  7.2 0.7 all-gather.13.cloned.1.call-update
  7.9 0.0 all-gather.9.cloned.1.call-start
  7.9 0.7 multiply_bitcast_fusion
  8.6 0.1 add_bitcast_fusion
  8.7 0.1 compare_and_fusion.2
  8.8 71.3 %all-gather.13.cloned.1.call-done = bf16[1,2048,1024]{2,1,0:T(8,128)(2,1)} async-done(((bf16[1,128,1024]{2,1,0:T(8,128)(2,1)}), bf16[1,2048,1024]{2,1,0:T(8,128)(2,1)}) %all-gather.13.cloned.1.call-update) | async-done | bytes 4194320 | tf_op jit(solution)/shard_map/all_gather | solution.py:43
  80.1 3.8 gather_fusion
  83.8 0.2 fusion.24
  84.1 3.9 convolution_convert_fusion.2
  88.1 0.8 fusion.32
  88.9 0.0 all-gather.11.cloned.1.call-start
  89.0 0.7 all-gather.11.cloned.1.call-update
  89.7 0.0 reduce-scatter.7.cloned.1.call-start
  89.7 25.4 %all-gather.1 = bf16[1,2048]{1,0:T(2,128)(2,1)S(1)} all-gather(bf16[1,128]{1,0:T(2,128)(2,1)S(1)} %convert_element_type.52), channel_id=3, replica_groups=mesh['seq'=16,'dp'=16] {'seq'}, dimensions={1}, use_global_device_ids=true | all-gather | bytes 4352 | tf_op jit(solution)/shard_map/all_gather | solution.py:44
  115.2 1.3 gather_fusion.1
  116.5 24.9 %all-gather.3 = bf16[16,1,128]{2,1,0:T(2,128)(2,1)S(1)} all-gather(bf16[1,1,128]{2,1,0:T(2,128)(2,1)S(1)} %select_bitcast_fusion), channel_id=1, replica_groups=mesh['seq'=16,'dp'=16] {'seq'}, dimensions={0}, use_global_device_ids=true | all-gather | bytes 4352 | tf_op jit(solution)/shard_map/all_gather | solution.py:59
  141.5 0.1 dynamic_slice.7
  141.5 0.2 copy.28
  141.7 0.3 compare_and_fusion
  142.0 0.2 copy.40
  142.2 21.2 %all-gather.9.cloned.1.call-done = bf16[2048,1024]{1,0:T(8,128)(2,1)} async-done(((bf16[128,1024]{1,0:T(8,128)(2,1)}), bf16[2048,1024]{1,0:T(8,128)(2,1)}) %all-gather.9.cloned.1.call-update) | async-done | bytes 4194320 | tf_op jit(solution)/shard_map/all_gather | solution.py:57
  163.4 6.5 %copy.39 = bf16[2048,1024]{0,1:T(8,128)(2,1)} copy(bf16[2048,1024]{1,0:T(8,128)(2,1)} %all-gather.9.cloned.1.call-done) | data formatting | bytes 8388608 | tf_op jit(solution)/shard_map/while/body/eval_jaxpr/reshape | solution.py:70
  169.9 5.1 fusion.2
  175.0 3.2 copy-done
  178.2 4.5 convolution_convert_fusion.1
  182.8 55.8 %all-gather.11.cloned.1.call-done = bf16[2048,1024]{1,0:T(8,128)(2,1)} async-done(((bf16[128,1024]{1,0:T(8,128)(2,1)}), bf16[2048,1024]{1,0:T(8,128)(2,1)}) %all-gather.11.cloned.1.call-update) | async-done | bytes 4194320 | tf_op jit(solution)/shard_map/all_gather | solution.py:58
  238.5 6.5 %copy.41 = bf16[2048,1024]{0,1:T(8,128)(2,1)} copy(bf16[2048,1024]{1,0:T(8,128)(2,1)} %all-gather.11.cloned.1.call-done) | data formatting | bytes 8388608 | tf_op jit(solution)/shard_map/while/body/eval_jaxpr/reshape | solution.py:71
  245.0 7.3 %fusion.13 = f32[128,8]{0,1:T(8,128)S(1)} fusion(bf16[2048,8,128]{0,2,1:T(8,128)(2,1)} %bitcast.52, bf16[128,8,128]{0,2,1:T(8,128)(2,1)S(1)} %bitcast.61, f32[8,128,2048]{2,1,0:T(8,128)} %copy-done, f32[8,128]{1,0:T(8,128)S(1)} %get-tuple-element.73, pred[128,2048]{1,0:T(8,128)(4,1)S(1)} %compare_and_fusion), kind=kOutput, calls=%fused_computation.20 | convolution fusion | flops 545651712 | bytes 13115392 | tf_op jit(solution)/shard_map/while/body/eval_jaxpr/hqk,khd->qhd/dot_general | solution.py:99
  252.3 5.2 fusion
  257.6 2.0 copy-done.2
  259.5 3.2 multiply_convert_fusion
  262.7 8.3 %pad_maximum_fusion = bf16[2048,2048]{0,1:T(8,128)(2,1)} fusion(bf16[2048,1024]{0,1:T(8,128)(2,1)} %bitcast.54, bf16[2048,1024]{0,1:T(8,128)(2,1)} %bitcast.50), kind=kLoop, calls=%fused_computation.2 | loop fusion | flops 16777216 | bytes 16777216 | tf_op jit(solution)/shard_map/while/body/eval_jaxpr/concatenate | solution.py:137
  271.1 12.2 %copy.37 = bf16[2048,2048]{1,0:T(8,128)(2,1)} copy(bf16[2048,2048]{0,1:T(8,128)(2,1)} %pad_maximum_fusion) | data formatting | bytes 16777216
  283.3 0.0 reduce-scatter.7.cloned.1.call-update
  283.3 0.3 reduce-scatter.5.cloned.1.call-start
  283.6 4.7 fusion.12
  288.3 103.2 %reduce-scatter.7.cloned.1.call-done = bf16[128,2048]{1,0:T(8,128)(2,1)} async-done(((bf16[2048,2048]{1,0:T(8,128)(2,1)}), bf16[128,2048]{1,0:T(8,128)(2,1)}) %reduce-scatter.7.cloned.1.call-update) | async-done | bytes 524304
  391.6 1.3 copy.38
  392.9 4.6 convolution_convert_fusion
  397.5 0.0 reduce-scatter.5.cloned.1.call-update
  397.6 0.0 all-gather.15.cloned.1.call-start
  397.6 76.1 %reduce-scatter.5.cloned.1.call-done = bf16[64,3072]{1,0:T(8,128)(2,1)} async-done(((bf16[1024,3072]{1,0:T(8,128)(2,1)}), bf16[64,3072]{1,0:T(8,128)(2,1)}) %reduce-scatter.5.cloned.1.call-update) | async-done | bytes 393232 | tf_op jit(solution)/shard_map/reduce_scatter | solution.py:171
  473.8 5.1 fusion.20
  478.9 0.9 fusion.25
  479.8 71.8 %all-gather.15.cloned.1.call-done = bf16[1024,3072]{1,0:T(8,128)(2,1)} async-done(((bf16[64,3072]{1,0:T(8,128)(2,1)}), bf16[1024,3072]{1,0:T(8,128)(2,1)}) %all-gather.15.cloned.1.call-update) | async-done | bytes 6291472 | tf_op jit(solution)/shard_map/all_gather | solution.py:13
  551.6 4.0 reduce_sum.53
  555.6 0.9 convert_multiply_fusion
  (21 shorter events, 0.2 us)
Async XLA Ops:
  7.2 72.9 %all-gather.13.cloned.1.call-start = ((), (), s32[]{:S(2)}) async-start(), calls=%async_computation.5 | async-start | bytes 4456448 | tf_op jit(solution)/shard_map/all_gather | solution.py:43
  7.9 155.5 %all-gather.9.cloned.1.call-start = ((), (), s32[]{:S(2)}) async-start(), calls=%async_computation.2 | async-start | bytes 4456448 | tf_op jit(solution)/shard_map/all_gather | solution.py:57
  84.1 5.6 copy-start.5
  84.1 57.4 %copy-start.3 = (bf16[1,128,1024]{2,1,0:T(8,128)(2,1)S(1)}, bf16[1,128,1024]{2,1,0:T(8,128)(2,1)}, u32[]{:S(2)}) copy-start(bf16[1,128,1024]{2,1,0:T(8,128)(2,1)} %param.11) | copy-start | bytes 786436
  88.9 149.6 %all-gather.11.cloned.1.call-start = ((), (), s32[]{:S(2)}) async-start(), calls=%async_computation.3 | async-start | bytes 4456448 | tf_op jit(solution)/shard_map/all_gather | solution.py:58
  89.7 301.9 %reduce-scatter.7.cloned.1.call-start = ((), (), s32[]{:S(2)}) async-start(), calls=%async_computation.7 | async-start | bytes 8912896
  175.0 3.2 copy-start
  245.0 7.3 %copy-start.1 = (f32[8,128,2048]{2,1,0:T(8,128)S(1)}, f32[8,128,2048]{2,1,0:T(8,128)}, u32[]{:S(2)}) copy-start(f32[8,128,2048]{2,1,0:T(8,128)} %copy-done) | copy-start | bytes 25165828
  257.6 2.0 copy-start.2
  283.3 109.6 %copy-start.4 = (f32[1024]{0:T(1024)S(1)}, f32[1024]{0:T(1024)}, u32[]{:S(2)}) copy-start(f32[1024]{0:T(1024)} %param.9) | copy-start | bytes 12292
  283.3 190.4 %reduce-scatter.5.cloned.1.call-start = ((), (), s32[]{:S(2)}) async-start(), calls=%async_computation.4 | async-start | bytes 6684672 | tf_op jit(solution)/shard_map/reduce_scatter | solution.py:171
  397.6 154.0 %all-gather.15.cloned.1.call-start = ((), (), s32[]{:S(2)}) async-start(), calls=%async_computation.6 | async-start | bytes 6684672 | tf_op jit(solution)/shard_map/all_gather | solution.py:13
Sparse Core Ops, SparseCore 0:
  9.8 70.2 all-gather.12
  89.0 74.2 all-gather.8
  165.7 72.7 all-gather.10
  283.5 108.0 reduce-scatter.6
  397.7 76.0 reduce-scatter.4
  476.3 75.2 all-gather.14
